TPU v7x, 32 devices: a whole 2x2x4 slice. The times are simulated.
32 devices in a mesh: expert: 8 (over y, x, core), dp: 4 (over z).
Axes of the slice: x: 2, y: 2, z: 4, core: 2. Of those that a mesh axis runs over, the one named last changes fastest.
Arguments:
- tokens: bfloat16 [4096, 2048], P(('expert', 'dp')), may hold values from -6 to 6
- expert_ids: int32 [4096, 8], P(('expert', 'dp')), may hold values from 0 to 15, all different within a row; in each aligned block of 128 rows (0 to 127, 128 to 255, ...) at most 72 rows name the same one
- router: bfloat16 [2048, 16], replicated, may hold values from -0.25 to 0.25
- w_gate: bfloat16 [16, 2048, 640], P('expert'), may hold values from -0.125 to 0.125
- w_up: bfloat16 [16, 2048, 640], P('expert'), may hold values from -0.125 to 0.125
- w_down: bfloat16 [16, 640, 2048], P('expert'), may hold values from -1 to 1
- out_grad: bfloat16 [4096, 2048], P(('expert', 'dp')), may hold values from -6 to 6
Outputs:
- mixed: bfloat16 [4096, 2048], P(('expert', 'dp'))
- token_grad: bfloat16 [4096, 2048], P(('expert', 'dp'))
- router_grad: float32 [2048, 16], replicated
- gate_grad: bfloat16 [16, 2048, 640], P('expert', 'dp')
- up_grad: bfloat16 [16, 2048, 640], P('expert', 'dp')
- down_grad: bfloat16 [16, 640, 2048], P('expert', None, 'dp')
Inputs may be any that keep to these rules, and one draw needn't show every extreme that they name: `expert_ids`: each row names 8 different experts; within the 128 rows of one device no expert is named more than 72 times.
All inputs are finite; a program needn't handle non-finite values.
Results may differ from a plain program's by a relative error of at most 0.008.
Values may be sent and summed in bfloat16 or wider, within the bound.
No kernel may reach another device: no remote copies, remote signals or barrier semaphores. Data moves between devices by JAX's collectives and lax.ppermute only.
A program may use at most 256 MiB of HBM per device.

v0:
```python
import jax
import jax.numpy as jnp
from jax import lax
from jax.sharding import PartitionSpec as P


def flat_rows(array):
    return array.reshape(array.shape[0], array.shape[1] * array.shape[2], array.shape[3])


def body(tokens, expert_ids, router, w_gate, w_up, w_down, out_grad):
    f32 = jnp.float32
    bf16 = jnp.bfloat16
    tok_dev, width = tokens.shape
    top = expert_ids.shape[1]
    n_experts = router.shape[1]
    local_experts = w_gate.shape[0]
    groups = lax.axis_size("expert")
    capacity = (tok_dev * top * 9 + 8 * n_experts - 1) // (8 * n_experts)
    n_assign = tok_dev * top
    flat_ids = expert_ids.reshape(-1)
    ladder = jnp.arange(n_experts, dtype=jnp.int32)
    onehot = (flat_ids[:, None] == ladder[None, :]).astype(jnp.int32)
    rank = jnp.sum((jnp.cumsum(onehot, axis=0) - onehot) * onehot, axis=1)
    owner = flat_ids // local_experts
    within = flat_ids % local_experts
    dest = (within * groups + owner) * capacity + rank
    slot_src = jnp.full((n_experts * capacity,), n_assign, jnp.int32)
    slot_src = slot_src.at[dest].set(jnp.arange(n_assign, dtype=jnp.int32))
    live = slot_src < n_assign
    slot_tok = jnp.where(live, slot_src // top, 0)
    logits = jnp.dot(tokens, router, preferred_element_type=f32)
    scores = jax.nn.sigmoid(logits)
    chosen = jnp.take_along_axis(scores, expert_ids, axis=1)
    total = jnp.sum(chosen, axis=1, keepdims=True)
    gates = chosen / total
    gate_slots = jnp.where(live, gates.reshape(-1)[jnp.minimum(slot_src, n_assign - 1)], 0.0)
    send = jnp.where(live[:, None], tokens[slot_tok], jnp.zeros((), bf16))
    send = send.reshape(local_experts, groups, capacity, width)
    piece = lax.all_to_all(send, "expert", split_axis=1, concat_axis=1, tiled=True)
    shape = piece.shape
    rows = flat_rows(piece)
    pre_gate = jnp.einsum("jrd,jdf->jrf", rows, w_gate, preferred_element_type=f32)
    pre_up = jnp.einsum("jrd,jdf->jrf", rows, w_up, preferred_element_type=f32)
    hidden = (pre_gate * jax.nn.sigmoid(pre_gate) * pre_up).astype(bf16)
    expert_out = jnp.einsum("jrf,jfd->jrd", hidden, w_down, preferred_element_type=f32).astype(bf16)
    hid_shape = (shape[0], shape[1], shape[2], hidden.shape[2])
    expert_out = expert_out.reshape(shape)
    hidden = hidden.reshape(hid_shape)
    results = (expert_out, hidden, piece, pre_gate.reshape(hid_shape), pre_up.reshape(hid_shape))
    expert_out = results[0]
    hidden = flat_rows(results[1])
    back = lax.all_to_all(expert_out, "expert", split_axis=1, concat_axis=1, tiled=True).reshape(
        n_experts * capacity, width
    )
    picked = back[dest].reshape(tok_dev, top, width)
    mixed = jnp.einsum("tk,tkd->td", gates, picked.astype(f32)).astype(bf16)
    gate_sens = jnp.einsum("tkd,td->tk", picked, out_grad, preferred_element_type=f32)
    grad_rows = (gate_slots[:, None] * out_grad[slot_tok].astype(f32)).astype(bf16)
    grad_send = jnp.where(live[:, None], grad_rows, jnp.zeros((), bf16))
    grad_send = grad_send.reshape(local_experts, groups, capacity, width)
    grad_in4 = lax.all_to_all(grad_send, "expert", split_axis=1, concat_axis=1, tiled=True)
    grad_in = flat_rows(grad_in4)
    pre_gate = flat_rows(results[3])
    pre_up = flat_rows(results[4])
    hidden_grad = jnp.einsum("jrd,jfd->jrf", grad_in, w_down, preferred_element_type=f32)
    sig = jax.nn.sigmoid(pre_gate)
    silu_val = pre_gate * sig
    gate_term = (hidden_grad * pre_up * sig * (1.0 + pre_gate * (1.0 - sig))).astype(bf16)
    up_term = (hidden_grad * silu_val).astype(bf16)
    input_grad = (
        jnp.einsum("jrf,jdf->jrd", gate_term, w_gate, preferred_element_type=f32)
        + jnp.einsum("jrf,jdf->jrd", up_term, w_up, preferred_element_type=f32)
    ).astype(bf16)
    input_grad = input_grad.reshape(grad_in4.shape)
    returned = lax.all_to_all(
        input_grad, "expert", split_axis=1, concat_axis=1, tiled=True
    ).reshape(n_experts * capacity, width)
    moe_grad = jnp.sum(returned[dest].reshape(tok_dev, top, width).astype(f32), axis=1)
    chosen_grad = (gate_sens - jnp.sum(gate_sens * gates, axis=1, keepdims=True)) / total
    sel_grad = chosen_grad * chosen * (1.0 - chosen)
    pick = (expert_ids[:, :, None] == ladder[None, None, :]).astype(f32)
    logit_grad = jnp.einsum("tk,tke->te", sel_grad, pick).astype(bf16)
    token_grad = (moe_grad + jnp.dot(logit_grad, router.T, preferred_element_type=f32)).astype(bf16)
    router_grad = lax.psum(
        jnp.dot(tokens.T, logit_grad, preferred_element_type=f32), ("expert", "dp")
    )
    hidden_width = hidden.shape[2]
    arrived4 = results[2]
    columns = (
        lax.all_to_all(arrived4, "dp", split_axis=3, concat_axis=1, tiled=True),
        lax.all_to_all(grad_in4, "dp", split_axis=3, concat_axis=1, tiled=True),
    )
    hid_shape = (local_experts, groups, capacity, hidden_width)
    hiddens = (
        lax.all_gather(gate_term.reshape(hid_shape), "dp", axis=1, tiled=True),
        lax.all_gather(up_term.reshape(hid_shape), "dp", axis=1, tiled=True),
        lax.all_gather(results[1], "dp", axis=1, tiled=True),
    )
    x_cols = flat_rows(columns[0])
    g_cols = flat_rows(columns[1])
    gate_grad = jnp.einsum(
        "jrd,jrf->jdf", x_cols, flat_rows(hiddens[0]), preferred_element_type=f32
    ).astype(bf16)
    up_grad = jnp.einsum(
        "jrd,jrf->jdf", x_cols, flat_rows(hiddens[1]), preferred_element_type=f32
    ).astype(bf16)
    down_grad = jnp.einsum(
        "jrf,jrd->jfd", flat_rows(hiddens[2]), g_cols, preferred_element_type=f32
    ).astype(bf16)
    return (mixed, token_grad, router_grad, gate_grad, up_grad, down_grad)


def solution(mesh):
    placed = (
        P(("expert", "dp"), None),
        P(("expert", "dp"), None),
        P(),
        P("expert", None, None),
        P("expert", None, None),
        P("expert", None, None),
        P(("expert", "dp"), None),
    )
    return jax.shard_map(
        body,
        mesh=mesh,
        in_specs=placed,
        out_specs=(
            P(("expert", "dp"), None),
            P(("expert", "dp"), None),
            P(),
            P("expert", "dp", None),
            P("expert", "dp", None),
            P("expert", None, "dp"),
        ),
        check_vma=False,
    )
```

profile of v0, /device:TPU:0, one launch (start us, length us, event | category | flops | bytes accessed | tf_op | source)
XLA Modules:
  0.0 936.1 jit_solution(13658574191496700082)
XLA Ops:
  18.7 6.0 gather_fusion
  27.4 59.9 %all_to_all.50 = bf16[2,8,72,2048]{3,2,0,1:T(8,128)(2,1)S(1)} all-to-all(bf16[2,8,72,2048]{3,2,0,1:T(8,128)(2,1)S(1)} %copy_select_fusion), channel_id=1, replica_groups=mesh['expert'=8,'dp'=4] {'expert'}, dimensions={1} | all-to-all | bytes 9437184 | tf_op jit(solution)/shard_map/all_to_all | solution.py:40
  93.6 5.7 multiply_convert_fusion.2
  106.0 4.7 all-to-all-start.1
  111.9 7.0 gather_fusion.5
  119.1 5.9 gather_fusion.3
  125.1 40.4 %all-to-all-done.1 = bf16[2,8,72,2048]{3,2,0,1:T(8,128)(2,1)} async-done(((bf16[2,8,72,2048]{3,2,0,1:T(8,128)(2,1)}), bf16[2,8,72,2048]{3,2,0,1:T(8,128)(2,1)}, u32[]{:S(2)}, u32[]{:S(2)}) %all-to-all-start.1) | async-done | bytes 4718624 | tf_op jit(solution)/shard_map/all_to_all | solution.py:53
  165.4 5.2 copy.117
  170.6 11.8 %gather_fusion.1 = bf16[1024,2048]{1,0:T(8,128)(2,1)} fusion(bf16[1152,2048]{1,0:T(8,128)(2,1)} %bitcast.104, s32[1024]{0:T(1024)S(1)} %broadcast_clamp_fusion), kind=kCustom, calls=%fused_computation.1 | custom fusion | bytes 8392704 | tf_op jit(solution)/shard_map/gather | solution.py:56
  182.4 4.9 fusion.2
  201.3 11.7 %copy.125 = bf16[2,8,72,2048]{2,1,0,3:T(8,128)(2,1)} copy(bf16[2,8,72,2048]{3,2,0,1:T(8,128)(2,1)} %copy-done.3) | data formatting | bytes 9437184 | tf_op jit(solution)/shard_map/all_to_all | solution.py:40
  213.0 43.1 %all-to-all-done.2 = bf16[2,8,72,2048]{3,2,0,1:T(8,128)(2,1)} async-done(((bf16[2,8,72,2048]{3,2,0,1:T(8,128)(2,1)}), bf16[2,8,72,2048]{3,2,0,1:T(8,128)(2,1)}, u32[]{:S(2)}, u32[]{:S(2)}) %all-to-all-start.2) | async-done | bytes 4718624 | tf_op jit(solution)/shard_map/all_to_all | solution.py:62
  256.1 5.6 all-to-all-start.4
  266.1 8.5 multiply_convert_fusion
  274.6 11.3 %fusion.34 = f32[2,576,2048]{2,1,0:T(8,128)} fusion(bf16[2,576,640]{2,1,0:T(8,128)(2,1)} %get-tuple-element.11, bf16[2,2048,640]{2,1,0:T(8,128)(2,1)} %param.10), kind=kOutput, calls=%fused_computation.86 | convolution fusion | flops 3019898880 | bytes 16154624 | tf_op jit(solution)/shard_map/jrf,jdf->jrd/dot_general | solution.py:72
  285.9 8.1 add_convert_fusion
  296.5 240.4 %all-to-all-done.4 = bf16[2,8,72,2048]{2,1,0,3:T(8,128)(2,1)} async-done(((bf16[2,8,72,2048]{2,1,0,3:T(8,128)(2,1)}), bf16[2,8,72,2048]{2,1,0,3:T(8,128)(2,1)}, u32[]{:S(2)}, u32[]{:S(2)}) %all-to-all-start.4) | async-done | bytes 4718624 | tf_op jit(solution)/shard_map/all_to_all | solution.py:91
  536.9 5.0 all-to-all-start.3
  542.6 11.8 %copy.130 = bf16[2,8,72,2048]{2,1,0,3:T(8,128)(2,1)} copy(bf16[2,8,72,2048]{3,2,0,1:T(8,128)(2,1)} %all-to-all-done.2) | data formatting | bytes 9437184 | tf_op jit(solution)/shard_map/all_to_all | solution.py:62
  554.4 42.3 %all-to-all-done.3 = bf16[2,8,72,2048]{3,2,0,1:T(8,128)(2,1)} async-done(((bf16[2,8,72,2048]{3,2,0,1:T(8,128)(2,1)}), bf16[2,8,72,2048]{3,2,0,1:T(8,128)(2,1)}, u32[]{:S(2)}, u32[]{:S(2)}) %all-to-all-start.3) | async-done | bytes 4718624 | tf_op jit(solution)/shard_map/all_to_all | solution.py:76
  596.7 5.6 all-to-all-start.5
  608.7 10.7 %copy.142 = bf16[2,8,72,4,512]{4,3,2,1,0:T(4,128)(2,1)} copy(bf16[2,8,72,4,512]{2,1,0,4,3:T(8,128)(2,1)} %bitcast.23) | data formatting | bytes 9437184 | tf_op jit(solution)/shard_map/all_to_all | solution.py:91
  619.4 5.5 copy.127
  624.9 5.3 copy.123
  630.2 11.8 %gather_fusion.4 = bf16[1024,2048]{1,0:T(8,128)(2,1)} fusion(bf16[1152,2048]{1,0:T(8,128)(2,1)} %bitcast.103, s32[1024]{0:T(1024)S(1)} %broadcast_clamp_fusion), kind=kCustom, calls=%fused_computation.4 | custom fusion | bytes 8392704 | tf_op jit(solution)/shard_map/gather | solution.py:79
  641.9 5.0 convert_reduce_fusion
  648.0 185.0 %all-to-all-done.5 = bf16[2,8,72,2048]{2,1,0,3:T(8,128)(2,1)} async-done(((bf16[2,8,72,2048]{2,1,0,3:T(8,128)(2,1)}), bf16[2,8,72,2048]{2,1,0,3:T(8,128)(2,1)}, u32[]{:S(2)}, u32[]{:S(2)}) %all-to-all-start.5) | async-done | bytes 4718624 | tf_op jit(solution)/shard_map/all_to_all | solution.py:92
  833.0 13.3 %copy.131 = bf16[2,8,72,4,512]{4,2,1,3,0:T(8,128)(2,1)} copy(bf16[2,8,72,4,512]{2,1,0,4,3:T(8,128)(2,1)} %bitcast.32) | data formatting | bytes 9437184 | tf_op jit(solution)/shard_map/all_to_all | solution.py:92
  846.4 8.4 convolution_convert_fusion.1
  854.8 9.1 convolution_convert_fusion.3
  863.9 9.2 convolution_convert_fusion.2
  873.1 53.9 %all-reduce.2.cloned.1.call-done = f32[2048,16]{0,1:T(8,128)} async-done(((f32[2048,16]{0,1:T(8,128)}), f32[2048,16]{0,1:T(8,128)}) %all-reduce.2.cloned.1.call-update) | async-done | bytes 131088 | tf_op jit(solution)/shard_map/psum | solution.py:85
  (106 shorter events, 58.0 us)
Async XLA Ops:
  8.0 111.1 %copy-start = (bf16[128,2048]{1,0:T(8,128)(2,1)S(1)}, bf16[128,2048]{1,0:T(8,128)(2,1)}, u32[]{:S(2)}) copy-start(bf16[128,2048]{1,0:T(8,128)(2,1)} %param.13) | copy-start | bytes 1572868
  8.0 10.7 %copy-start.2 = (bf16[128,2048]{1,0:T(8,128)(2,1)S(1)}, bf16[128,2048]{1,0:T(8,128)(2,1)}, u32[]{:S(2)}) copy-start(bf16[128,2048]{1,0:T(8,128)(2,1)} %param.7) | copy-start | bytes 1572868
  8.9 15.8 %copy-start.6 = (s32[128,8]{1,0:T(8,128)}, s32[128,8]{1,0:T(8,128)S(1)}, u32[]{:S(2)}) copy-start(s32[128,8]{1,0:T(8,128)S(1)} %copy.108) | copy-start | bytes 12292
  27.4 62.3 %slice-start.2 = ((s8[5242880]{0:T(1024)(128)(4,1)}), s8[4194304]{0:T(1024)(128)(4,1)S(1)}, s32[]{:S(2)}) async-start(s8[5242880]{0:T(1024)(128)(4,1)} %bitcast.133), calls=%async_computation.12 | async-start | bytes 8388608
  87.3 2.4 copy-start.3
  87.3 2.4 slice-start.3
  87.3 6.3 slice-start.4
  89.7 3.9 slice-start.5
  89.7 9.6 %slice-start = ((s8[5242880]{0:T(1024)(128)(4,1)}), s8[4194304]{0:T(1024)(128)(4,1)S(1)}, s32[]{:S(2)}) async-start(s8[5242880]{0:T(1024)(128)(4,1)} %bitcast.131), calls=%async_computation.10 | async-start | bytes 8388608
  93.6 5.7 copy-start.10
  93.6 5.7 slice-start.1
  99.3 4.1 copy-start.4
  106.0 5.5 copy-start.9
  106.0 5.7 copy-start.8
  106.0 59.5 %all-to-all-start.1 = ((bf16[2,8,72,2048]{3,2,0,1:T(8,128)(2,1)}), bf16[2,8,72,2048]{3,2,0,1:T(8,128)(2,1)}, u32[]{:S(2)}, u32[]{:S(2)}) async-start(bf16[2,8,72,2048]{3,2,0,1:T(8,128)(2,1)} %copy.116), calls=%async_computation.1 | async-start | bytes 9437184 | tf_op jit(solution)/shard_map/all_to_all | solution.py:53
  110.7 735.7 %all-gather.8.cloned.1.call-start = ((), (), s32[]{:S(2)}) async-start(), calls=%async_computation.9 | async-start | bytes 7372800 | tf_op jit(solution)/shard_map/all_gather | solution.py:98
  196.7 59.4 %all-to-all-start.2 = ((bf16[2,8,72,2048]{3,2,0,1:T(8,128)(2,1)}), bf16[2,8,72,2048]{3,2,0,1:T(8,128)(2,1)}, u32[]{:S(2)}, u32[]{:S(2)}) async-start(bf16[2,8,72,2048]{3,2,0,1:T(8,128)(2,1)} %fusion.1), calls=%async_computation.2 | async-start | bytes 9437184 | tf_op jit(solution)/shard_map/all_to_all | solution.py:62
  256.1 280.8 %all-to-all-start.4 = ((bf16[2,8,72,2048]{2,1,0,3:T(8,128)(2,1)}), bf16[2,8,72,2048]{2,1,0,3:T(8,128)(2,1)}, u32[]{:S(2)}, u32[]{:S(2)}) async-start(bf16[2,8,72,2048]{2,1,0,3:T(8,128)(2,1)} %copy.125), calls=%async_computation.4 | async-start | bytes 16777216 | tf_op jit(solution)/shard_map/all_to_all | solution.py:91
  261.7 593.1 %all-gather.4.cloned.1.call-start = ((), (), s32[]{:S(2)}) async-start(), calls=%async_computation.7 | async-start | bytes 7372800 | tf_op jit(solution)/shard_map/all_gather | solution.py:96
  261.9 3.3 copy-start.11
  261.9 4.1 copy-start.12
  274.5 11.3 %copy-start.5 = (bf16[2,576,640]{2,1,0:T(8,128)(2,1)}, bf16[2,576,640]{2,1,0:T(8,128)(2,1)S(1)}, u32[]{:S(2)}) copy-start(bf16[2,576,640]{2,1,0:T(8,128)(2,1)S(1)} %get-tuple-element.10) | copy-start | bytes 4423684
  536.9 59.8 %all-to-all-start.3 = ((bf16[2,8,72,2048]{3,2,0,1:T(8,128)(2,1)}), bf16[2,8,72,2048]{3,2,0,1:T(8,128)(2,1)}, u32[]{:S(2)}, u32[]{:S(2)}) async-start(bf16[2,8,72,2048]{3,2,0,1:T(8,128)(2,1)} %copy.122), calls=%async_computation.3 | async-start | bytes 9437184 | tf_op jit(solution)/shard_map/all_to_all | solution.py:76
  541.8 322.1 %all-gather.6.cloned.1.call-start = ((), (), s32[]{:S(2)}) async-start(), calls=%async_computation.8 | async-start | bytes 7372800 | tf_op jit(solution)/shard_map/all_gather | solution.py:97
  596.7 236.3 %all-to-all-start.5 = ((bf16[2,8,72,2048]{2,1,0,3:T(8,128)(2,1)}), bf16[2,8,72,2048]{2,1,0,3:T(8,128)(2,1)}, u32[]{:S(2)}, u32[]{:S(2)}) async-start(bf16[2,8,72,2048]{2,1,0,3:T(8,128)(2,1)} %copy.130), calls=%async_computation.5 | async-start | bytes 16777216 | tf_op jit(solution)/shard_map/all_to_all | solution.py:92
  602.3 5.1 copy-start.7
  602.3 324.6 %all-reduce.2.cloned.1.call-start = ((), (), s32[]{:S(2)}) async-start(), calls=%async_computation.6 | async-start | bytes 262144 | tf_op jit(solution)/shard_map/psum | solution.py:85
  863.9 64.6 %copy-start.1 = (bf16[128,2048]{1,0:T(8,128)(2,1)S(1)}, bf16[128,2048]{1,0:T(8,128)(2,1)}, u32[]{:S(2)}) copy-start(bf16[128,2048]{1,0:T(8,128)(2,1)} %param.13) | copy-start | bytes 1572868
Sparse Core Ops, SparseCore 0:
  113.1 110.4 all-gather.7
  274.7 221.0 all-gather.3
  544.3 178.8 all-gather.5
Sparse Core Ops, SparseCore 1:
  608.9 318.0 all-reduce.1
where the time goes:
time: 946 us; the launch traced here: 936 us
  waiting for transfers between devices  606 us (64%)
  local copies, waits for them, and re-layouts  132 us (14%)
  matrix products  79 us (8%)
  blocking collectives  59.9 us (6%)
  starting transfers between devices  26.6 us (3%)
  other arithmetic  17 us (2%)
  between operations  16.1 us (2%)
    all_to_all x1, waiting for transfers between devices, body(): lax.all_to_all(arrived4, 'dp', split_axis=3, concat_axis=1, tiled=True)  240 us
    all_to_all x1, waiting for transfers between devices, body(): lax.all_to_all(grad_in4, 'dp', split_axis=3, concat_axis=1, tiled=True)  185 us
    all_to_all x1, blocking collectives, body(): lax.all_to_all(send, 'expert', split_axis=1, concat_axis=1, tiled=True)  59.9 us
    psum x1, waiting for transfers between devices, body(): lax.psum(jnp.dot(tokens.T, logit_grad, preferred_element_type=f32), ('exp...  53.9 us
    all_to_all x1, waiting for transfers between devices, body(): lax.all_to_all(grad_send, 'expert', split_axis=1, concat_axis=1, tiled=True)  43.1 us
    all_to_all x1, waiting for transfers between devices, body(): lax.all_to_all(input_grad, 'expert', split_axis=1, concat_axis=1, tiled=T...  42.3 us
    all_to_all x1, waiting for transfers between devices, body(): lax.all_to_all(expert_out, 'expert', split_axis=1, concat_axis=1, tiled=T...  40.4 us
  transfers between devices with their start and end apart: 9, of which 6 were waited for; matrix products, arithmetic and copies ran while one was open for 20% of the time, Pallas kernels for 0%

commit v1 on v0

--- a/solution.py
+++ b/solution.py
@@ -82,8 +82,9 @@
     pick = (expert_ids[:, :, None] == ladder[None, None, :]).astype(f32)
     logit_grad = jnp.einsum("tk,tke->te", sel_grad, pick).astype(bf16)
     token_grad = (moe_grad + jnp.dot(logit_grad, router.T, preferred_element_type=f32)).astype(bf16)
-    router_grad = lax.psum(
-        jnp.dot(tokens.T, logit_grad, preferred_element_type=f32), ("expert", "dp")
+    router_grad = jnp.sum(
+        lax.all_gather(jnp.dot(tokens.T, logit_grad, preferred_element_type=f32), ("expert", "dp")),
+        axis=0,
     )
     hidden_width = hidden.shape[2]
     arrived4 = results[2]

time: 946 us -> 1010 us (1.068)
  waiting for transfers between devices: 606 us -> 664 us
    all_to_all x1, waiting for transfers between devices: 240 us -> 295 us  [body(): lax.all_to_all(arrived4, 'dp', split_axis=3, concat_axis=1, tiled=True)]
    psum x1 -> x0, waiting for transfers between devices: 53.9 us -> none  [body(): lax.psum(jnp.dot(tokens.T, logit_grad, preferred_element_type=f32), ('exp...]
    all_to_all x1, waiting for transfers between devices: 185 us -> 224 us  [body(): lax.all_to_all(grad_in4, 'dp', split_axis=3, concat_axis=1, tiled=True)]
    all_to_all x1, waiting for transfers between devices: 43.1 us -> 54.1 us  [body(): lax.all_to_all(grad_send, 'expert', split_axis=1, concat_axis=1, tiled=True)]
  transfers between devices with their start and end apart: 9 -> 9, of which waited for: 6 -> 5; matrix products, arithmetic and copies ran while one was open for 20% -> 16% of each run, Pallas kernels for 0% -> 0%
where the time goes in v1:
time: 1010 us; the launch traced here: 998 us
  waiting for transfers between devices  664 us (66%)
  local copies, waits for them, and re-layouts  135 us (13%)
  matrix products  79.1 us (8%)
  blocking collectives  59.9 us (6%)
  starting transfers between devices  27.5 us (3%)
  other arithmetic  18.2 us (2%)
  between operations  14.4 us (1%)
    all_to_all x1, waiting for transfers between devices, body(): lax.all_to_all(arrived4, 'dp', split_axis=3, concat_axis=1, tiled=True)  295 us
    all_to_all x1, waiting for transfers between devices, body(): lax.all_to_all(grad_in4, 'dp', split_axis=3, concat_axis=1, tiled=True)  224 us
    all_to_all x1, blocking collectives, body(): lax.all_to_all(send, 'expert', split_axis=1, concat_axis=1, tiled=True)  59.9 us
    all_to_all x1, waiting for transfers between devices, body(): lax.all_to_all(grad_send, 'expert', split_axis=1, concat_axis=1, tiled=True)  54.1 us
    all_to_all x1, waiting for transfers between devices, body(): lax.all_to_all(expert_out, 'expert', split_axis=1, concat_axis=1, tiled=T...  46.8 us
    all_to_all x1, waiting for transfers between devices, body(): lax.all_to_all(input_grad, 'expert', split_axis=1, concat_axis=1, tiled=T...  43.1 us
  transfers between devices with their start and end apart: 9, of which 5 were waited for; matrix products, arithmetic and copies ran while one was open for 16% of the time, Pallas kernels for 0%

profile of v1, /device:TPU:0, one launch (start us, length us, event | category | flops | bytes accessed | tf_op | source)
XLA Modules:
  0.0 998.0 jit_solution(15425907123020387887)
XLA Ops:
  17.9 6.0 gather_fusion
  26.6 59.9 %all_to_all.50 = bf16[2,8,72,2048]{3,2,0,1:T(8,128)(2,1)S(1)} all-to-all(bf16[2,8,72,2048]{3,2,0,1:T(8,128)(2,1)S(1)} %copy_select_fusion), channel_id=1, replica_groups=mesh['expert'=8,'dp'=4] {'expert'}, dimensions={1} | all-to-all | bytes 9437184 | tf_op jit(solution)/shard_map/all_to_all | solution.py:40
  92.8 5.6 multiply_convert_fusion.2
  105.1 4.8 all-to-all-start.1
  110.6 7.0 gather_fusion.5
  117.8 46.8 %all-to-all-done.1 = bf16[2,8,72,2048]{3,2,0,1:T(8,128)(2,1)} async-done(((bf16[2,8,72,2048]{3,2,0,1:T(8,128)(2,1)}), bf16[2,8,72,2048]{3,2,0,1:T(8,128)(2,1)}, u32[]{:S(2)}, u32[]{:S(2)}) %all-to-all-start.1) | async-done | bytes 4718624 | tf_op jit(solution)/shard_map/all_to_all | solution.py:53
  164.6 5.3 copy.117
  169.9 11.7 %gather_fusion.1 = bf16[1024,2048]{1,0:T(8,128)(2,1)} fusion(bf16[1152,2048]{1,0:T(8,128)(2,1)} %bitcast.109, s32[1024]{0:T(1024)S(1)} %broadcast_clamp_fusion), kind=kCustom, calls=%fused_computation.1 | custom fusion | bytes 8392704 | tf_op jit(solution)/shard_map/gather | solution.py:56
  181.6 4.9 fusion.2
  188.8 6.0 gather_fusion.3
  204.0 4.6 all-to-all-start.2
  208.6 11.7 %copy.125 = bf16[2,8,72,2048]{2,1,0,3:T(8,128)(2,1)} copy(bf16[2,8,72,2048]{3,2,0,1:T(8,128)(2,1)} %copy-done.3) | data formatting | bytes 9437184 | tf_op jit(solution)/shard_map/all_to_all | solution.py:40
  220.3 54.1 %all-to-all-done.2 = bf16[2,8,72,2048]{3,2,0,1:T(8,128)(2,1)} async-done(((bf16[2,8,72,2048]{3,2,0,1:T(8,128)(2,1)}), bf16[2,8,72,2048]{3,2,0,1:T(8,128)(2,1)}, u32[]{:S(2)}, u32[]{:S(2)}) %all-to-all-start.2) | async-done | bytes 4718624 | tf_op jit(solution)/shard_map/all_to_all | solution.py:62
  274.4 5.6 all-to-all-start.4
  284.3 9.1 multiply_convert_fusion
  293.4 10.9 %fusion.34 = f32[2,576,2048]{2,1,0:T(8,128)} fusion(bf16[2,576,640]{2,1,0:T(8,128)(2,1)} %get-tuple-element.11, bf16[2,2048,640]{2,1,0:T(8,128)(2,1)} %param.10), kind=kOutput, calls=%fused_computation.87 | convolution fusion | flops 3019898880 | bytes 16154624 | tf_op jit(solution)/shard_map/jrf,jdf->jrd/dot_general | solution.py:72
  304.3 8.1 add_convert_fusion
  314.9 294.9 %all-to-all-done.4 = bf16[2,8,72,2048]{2,1,0,3:T(8,128)(2,1)} async-done(((bf16[2,8,72,2048]{2,1,0,3:T(8,128)(2,1)}), bf16[2,8,72,2048]{2,1,0,3:T(8,128)(2,1)}, u32[]{:S(2)}, u32[]{:S(2)}) %all-to-all-start.4) | async-done | bytes 4718624 | tf_op jit(solution)/shard_map/all_to_all | solution.py:92
  614.5 11.7 %copy.130 = bf16[2,8,72,2048]{2,1,0,3:T(8,128)(2,1)} copy(bf16[2,8,72,2048]{3,2,0,1:T(8,128)(2,1)} %all-to-all-done.2) | data formatting | bytes 9437184 | tf_op jit(solution)/shard_map/all_to_all | solution.py:62
  626.1 43.1 %all-to-all-done.3 = bf16[2,8,72,2048]{3,2,0,1:T(8,128)(2,1)} async-done(((bf16[2,8,72,2048]{3,2,0,1:T(8,128)(2,1)}), bf16[2,8,72,2048]{3,2,0,1:T(8,128)(2,1)}, u32[]{:S(2)}, u32[]{:S(2)}) %all-to-all-start.3) | async-done | bytes 4718624 | tf_op jit(solution)/shard_map/all_to_all | solution.py:76
  669.2 7.2 all-to-all-start.5
  681.6 10.9 %copy.142 = bf16[2,8,72,4,512]{4,3,2,1,0:T(4,128)(2,1)} copy(bf16[2,8,72,4,512]{2,1,0,4,3:T(8,128)(2,1)} %bitcast.23) | data formatting | bytes 9437184 | tf_op jit(solution)/shard_map/all_to_all | solution.py:92
  692.5 5.4 copy.127
  698.0 4.6 copy.144
  703.7 5.3 copy.123
  709.0 11.8 %gather_fusion.4 = bf16[1024,2048]{1,0:T(8,128)(2,1)} fusion(bf16[1152,2048]{1,0:T(8,128)(2,1)} %bitcast.108, s32[1024]{0:T(1024)S(1)} %broadcast_clamp_fusion), kind=kCustom, calls=%fused_computation.4 | custom fusion | bytes 8392704 | tf_op jit(solution)/shard_map/gather | solution.py:79
  720.8 5.1 convert_reduce_fusion
  727.0 224.4 %all-to-all-done.5 = bf16[2,8,72,2048]{2,1,0,3:T(8,128)(2,1)} async-done(((bf16[2,8,72,2048]{2,1,0,3:T(8,128)(2,1)}), bf16[2,8,72,2048]{2,1,0,3:T(8,128)(2,1)}, u32[]{:S(2)}, u32[]{:S(2)}) %all-to-all-start.5) | async-done | bytes 4718624 | tf_op jit(solution)/shard_map/all_to_all | solution.py:93
  951.4 13.2 %copy.131 = bf16[2,8,72,4,512]{4,2,1,3,0:T(8,128)(2,1)} copy(bf16[2,8,72,4,512]{2,1,0,4,3:T(8,128)(2,1)} %bitcast.32) | data formatting | bytes 9437184 | tf_op jit(solution)/shard_map/all_to_all | solution.py:93
  964.6 8.4 convolution_convert_fusion.1
  973.0 9.1 convolution_convert_fusion.3
  982.1 9.1 convolution_convert_fusion.2
  (103 shorter events, 57.3 us)
Async XLA Ops:
  7.2 174.5 %copy-start = (bf16[128,2048]{1,0:T(8,128)(2,1)S(1)}, bf16[128,2048]{1,0:T(8,128)(2,1)}, u32[]{:S(2)}) copy-start(bf16[128,2048]{1,0:T(8,128)(2,1)} %param.13) | copy-start | bytes 1572868
  7.2 10.7 %copy-start.2 = (bf16[128,2048]{1,0:T(8,128)(2,1)S(1)}, bf16[128,2048]{1,0:T(8,128)(2,1)}, u32[]{:S(2)}) copy-start(bf16[128,2048]{1,0:T(8,128)(2,1)} %param.7) | copy-start | bytes 1572868
  26.6 62.3 %slice-start.2 = ((s8[5242880]{0:T(1024)(128)(4,1)}), s8[4194304]{0:T(1024)(128)(4,1)S(1)}, s32[]{:S(2)}) async-start(s8[5242880]{0:T(1024)(128)(4,1)} %bitcast.139), calls=%async_computation.12 | async-start | bytes 8388608
  86.5 2.4 copy-start.3
  86.5 2.4 slice-start.3
  86.5 6.3 slice-start.4
  88.9 3.9 slice-start.5
  88.9 9.5 slice-start
  92.8 5.6 copy-start.8
  92.8 5.6 slice-start.1
  98.4 4.1 copy-start.4
  105.1 5.0 copy-start.7
  105.1 5.2 copy-start.6
  105.1 59.5 %all-to-all-start.1 = ((bf16[2,8,72,2048]{3,2,0,1:T(8,128)(2,1)}), bf16[2,8,72,2048]{3,2,0,1:T(8,128)(2,1)}, u32[]{:S(2)}, u32[]{:S(2)}) async-start(bf16[2,8,72,2048]{3,2,0,1:T(8,128)(2,1)} %copy.116), calls=%async_computation.1 | async-start | bytes 9437184 | tf_op jit(solution)/shard_map/all_to_all | solution.py:53
  109.9 588.1 %all-gather.12.cloned.1.call-start = ((), (), s32[]{:S(2)}) async-start(), calls=%async_computation.9 | async-start | bytes 4325376 | tf_op jit(solution)/shard_map/all_gather | solution.py:86
  188.0 776.6 %all-gather.10.cloned.1.call-start = ((), (), s32[]{:S(2)}) async-start(), calls=%async_computation.8 | async-start | bytes 7372800 | tf_op jit(solution)/shard_map/all_gather | solution.py:99
  204.0 70.4 %all-to-all-start.2 = ((bf16[2,8,72,2048]{3,2,0,1:T(8,128)(2,1)}), bf16[2,8,72,2048]{3,2,0,1:T(8,128)(2,1)}, u32[]{:S(2)}, u32[]{:S(2)}) async-start(bf16[2,8,72,2048]{3,2,0,1:T(8,128)(2,1)} %fusion.1), calls=%async_computation.2 | async-start | bytes 9437184 | tf_op jit(solution)/shard_map/all_to_all | solution.py:62
  274.4 335.4 %all-to-all-start.4 = ((bf16[2,8,72,2048]{2,1,0,3:T(8,128)(2,1)}), bf16[2,8,72,2048]{2,1,0,3:T(8,128)(2,1)}, u32[]{:S(2)}, u32[]{:S(2)}) async-start(bf16[2,8,72,2048]{2,1,0,3:T(8,128)(2,1)} %copy.125), calls=%async_computation.4 | async-start | bytes 16777216 | tf_op jit(solution)/shard_map/all_to_all | solution.py:92
  280.1 692.9 %all-gather.6.cloned.1.call-start = ((), (), s32[]{:S(2)}) async-start(), calls=%async_computation.6 | async-start | bytes 7372800 | tf_op jit(solution)/shard_map/all_gather | solution.py:97
  280.1 3.3 copy-start.9
  280.1 4.2 copy-start.10
  293.4 11.0 %copy-start.5 = (bf16[2,576,640]{2,1,0:T(8,128)(2,1)}, bf16[2,576,640]{2,1,0:T(8,128)(2,1)S(1)}, u32[]{:S(2)}) copy-start(bf16[2,576,640]{2,1,0:T(8,128)(2,1)S(1)} %get-tuple-element.10) | copy-start | bytes 4423684
  609.9 59.3 %all-to-all-start.3 = ((bf16[2,8,72,2048]{3,2,0,1:T(8,128)(2,1)}), bf16[2,8,72,2048]{3,2,0,1:T(8,128)(2,1)}, u32[]{:S(2)}, u32[]{:S(2)}) async-start(bf16[2,8,72,2048]{3,2,0,1:T(8,128)(2,1)} %copy.122), calls=%async_computation.3 | async-start | bytes 9437184 | tf_op jit(solution)/shard_map/all_to_all | solution.py:76
  669.2 282.2 %all-to-all-start.5 = ((bf16[2,8,72,2048]{2,1,0,3:T(8,128)(2,1)}), bf16[2,8,72,2048]{2,1,0,3:T(8,128)(2,1)}, u32[]{:S(2)}, u32[]{:S(2)}) async-start(bf16[2,8,72,2048]{2,1,0,3:T(8,128)(2,1)} %copy.130), calls=%async_computation.5 | async-start | bytes 16777216 | tf_op jit(solution)/shard_map/all_to_all | solution.py:93
  676.4 305.7 %all-gather.8.cloned.1.call-start = ((), (), s32[]{:S(2)}) async-start(), calls=%async_computation.7 | async-start | bytes 7372800 | tf_op jit(solution)/shard_map/all_gather | solution.py:98
  982.1 9.1 copy-start.1
Sparse Core Ops, SparseCore 0:
  188.1 78.8 all-gather.11
  268.6 245.4 all-gather.9
  515.7 135.0 all-gather.5
  678.5 232.6 all-gather.7
